TPU v7x, 32 devices: a whole 2x2x4 slice. The times are simulated.
32 devices in a mesh: sub: 16 (over z, y, x), mode: 2 (over core).
Axes of the slice: x: 2, y: 2, z: 4, core: 2. Of those that a mesh axis runs over, the one named last changes fastest.
Arguments:
- coupling: bfloat16 [1024, 64, 128], P('sub'), may hold values from -0.5 to 0.5
- coupling_pairs: int32 [1024, 2], P('sub'), may hold values from 0 to 3, as said below
- modes: bfloat16 [1024, 256, 256], P('sub', None, 'mode'), may hold values from -6 to 6
- mode_weights: bfloat16 [1024, 256], P('sub', 'mode'), may hold values from 0 to 1, as said below
- parent_of: int32 [1024, 1], P('sub'), may hold values from 0 to 15; in each aligned block of 64 rows (0 to 63, 64 to 127, ...) at most 8 rows name the same one
- row_block: int32 [1024], P('sub'), may hold values from 0 to 7
- parent_modes: bfloat16 [16, 512, 256], P('sub'), may hold values from -1 to 1
- parent_eigs: float32 [16, 256], P('sub'), may hold values from 0.02 to 0.5
Outputs:
- strengths: float32 [1024, 256], P('sub', 'mode')
Inputs may be any that keep to these rules, and one draw needn't show every extreme that they name: `coupling_pairs`: within each child the 2 block indices are distinct. `parent_of`: the 64 children of one index of sub name any one parent at most 8 times; some parent is named exactly 8 times by some index's children. `mode_weights`: Positive.
All inputs are finite; a program needn't handle non-finite values.
Results may differ from a plain program's by a relative error of at most 0.0015.
Values may be sent and summed in bfloat16 or wider, within the bound.
A program may use at most 128 MiB of HBM per device.

v0:
```python
import jax
import jax.numpy as jnp
from jax import lax
from jax.sharding import PartitionSpec as P

M = 256
MP = 256
BLK = 64
CH_DEV = 64


def pick_blocks(modes, coupling_pairs):
    child_count, interface_rows, mode_cols = modes.shape
    blocks = modes.reshape(child_count, interface_rows // BLK, BLK, mode_cols)
    selector = (
        coupling_pairs[:, :, None]
        == jnp.arange(interface_rows // BLK, dtype=jnp.int32)[None, None, :]
    ).astype(jnp.bfloat16)
    picked = jnp.einsum(
        "skb,sbim->skim", selector, blocks, preferred_element_type=jnp.float32
    ).astype(jnp.bfloat16)
    return picked.reshape(child_count, coupling_pairs.shape[1] * BLK, mode_cols)


def weighted_records(coupling_rows, picked, weights):
    record = jnp.einsum("sij,sjm->sim", coupling_rows, picked, preferred_element_type=jnp.float32)
    return (record * weights[:, None, :].astype(jnp.float32)).astype(jnp.bfloat16)


def to_slots(values, slot_index, slot_count):
    empty = jnp.zeros((slot_count,) + values.shape[1:], values.dtype)
    return empty.at[slot_index].set(values)


def per_device(
    coupling, coupling_pairs, modes, mode_weights, parent_of, row_block, parent_modes, parent_eigs
):
    sub_count = lax.axis_size("sub")
    child_count = coupling.shape[0]
    mode_cols = modes.shape[2]
    capacity = max(2, 2 * child_count // sub_count)
    slot_count = sub_count * capacity
    owner = parent_of[:, 0]
    order_ids = jnp.arange(child_count, dtype=jnp.int32)
    earlier = (owner[:, None] == owner[None, :]) & (order_ids[None, :] < order_ids[:, None])
    position = jnp.sum(earlier.astype(jnp.int32), axis=1)
    slot_index = owner * capacity + position
    picked = pick_blocks(modes, coupling_pairs)
    row_send = to_slots(row_block, slot_index, slot_count).reshape(sub_count, capacity)
    record = weighted_records(coupling, picked, mode_weights)
    record_send = to_slots(record, slot_index, slot_count).reshape(
        sub_count, capacity, BLK, mode_cols
    )
    record_recv, row_recv = (
        lax.all_to_all(record_send, "sub", split_axis=0, concat_axis=0, tiled=True),
        lax.all_to_all(row_send, "sub", split_axis=0, concat_axis=0, tiled=True),
    )
    records = record_recv.reshape(slot_count, BLK, mode_cols)
    row_index = row_recv.reshape(slot_count)
    sep_blocks = parent_modes.shape[1] // BLK
    parent_blocks = parent_modes[0].reshape(sep_blocks, BLK, MP)
    group_size = min(64, slot_count)
    group_count = slot_count // group_size
    record_groups = records.reshape(group_count, group_size, BLK, mode_cols)
    row_groups = row_index.reshape(group_count, group_size)

    def project(gram_sum, members):
        record_part, row_part = members
        selector = (row_part[:, None] == jnp.arange(sep_blocks, dtype=jnp.int32)[None, :]).astype(
            jnp.bfloat16
        )
        parent_rows = jnp.einsum(
            "sb,bik->sik", selector, parent_blocks, preferred_element_type=jnp.float32
        ).astype(jnp.bfloat16)
        projected = jnp.einsum(
            "sik,sim->skm", parent_rows, record_part, preferred_element_type=jnp.float32
        ).astype(jnp.bfloat16)
        term = jnp.einsum("skm,slm->kl", projected, projected, preferred_element_type=jnp.float32)
        return (gram_sum + term, projected)

    gram_sum, projected_all = lax.scan(
        project, jnp.zeros((MP, MP), jnp.float32), (record_groups, row_groups)
    )
    gram_sum = lax.psum(gram_sum, "mode")
    pencil = jnp.diag(parent_eigs[0]) + gram_sum / (CH_DEV * M)
    factor = jnp.linalg.cholesky(pencil)
    identity = jnp.eye(MP, dtype=pencil.dtype)
    inverse = lax.linalg.triangular_solve(factor, identity, left_side=True, lower=True).astype(
        jnp.bfloat16
    )

    def strength(projected):
        rotated = jnp.einsum("kl,slm->skm", inverse, projected, preferred_element_type=jnp.float32)
        return jnp.sum(rotated * rotated, axis=1) / MP

    slot_values = lax.map(strength, projected_all).reshape(sub_count, capacity, mode_cols)
    returned = lax.all_to_all(slot_values, "sub", split_axis=0, concat_axis=0, tiled=True)
    return returned.reshape(slot_count, mode_cols)[slot_index]


def solution(mesh):
    in_specs = (
        P("sub", None, None),
        P("sub", None),
        P("sub", None, "mode"),
        P("sub", "mode"),
        P("sub", None),
        P("sub"),
        P("sub", None, None),
        P("sub", None),
    )
    out_specs = P("sub", "mode")
    return jax.shard_map(
        per_device, mesh=mesh, in_specs=in_specs, out_specs=out_specs, check_vma=False
    )
```

profile of v0, /device:TPU:0, one launch (start us, length us, event | category | flops | bytes accessed | tf_op | source)
XLA Modules:
  0.0 229.0 jit_solution(5430570650498612388)
XLA Ops:
  6.5 0.9 convert_reduce_fusion
  7.5 0.7 fusion.31
  8.1 0.9 scatter_custom_fusion
  9.1 0.7 all_to_all.12
  9.7 8.3 %all-to-all-start = ((s32[16,1,8]{2,1,0:T(1,128)}), s32[16,1,8]{2,1,0:T(1,128)S(1)}, u32[]{:S(2)}, u32[]{:S(2)}) async-start(s32[16,1,8]{2,1,0:T(1,128)} %bitcast.6), calls=%async_computation | async-start | bytes 16384 | tf_op jit(solution)/shard_map/all_to_all | solution.py:56
  18.1 0.8 copy.57
  18.9 5.6 %fusion.15 = bf16[64,2,64,128]{3,1,2,0:T(2,128)(2,1)S(1)} fusion(bf16[64,4,64,128]{3,2,1,0:T(8,128)(2,1)} %bitcast.113, s32[64,2]{1,0:T(8,128)S(1)} %copy.57), kind=kOutput, calls=%fused_computation.27 | convolution fusion | flops 9437696 | bytes 6291968 | tf_op jit(solution)/shard_map/skb,sbim->skim/dot_general | solution.py:19
  24.5 0.6 copy.59
  25.2 1.7 fusion.18
  26.9 0.5 broadcast_in_dim.55
  27.4 6.2 %scatter_fusion = bf16[128,64,128]{2,1,0:T(8,128)(2,1)S(1)} fusion(bf16[128,64,128]{2,1,0:T(8,128)(2,1)S(1)} %broadcast_in_dim.55, s32[64]{0:T(128)S(1)} %fusion.31, bf16[64,64,128]{2,1,0:T(8,128)(2,1)} %fusion.18), kind=kCustom, calls=%fused_computation.2 | custom fusion | bytes 3145984 | tf_op jit(solution)/shard_map/scatter | solution.py:32
  33.6 1.4 copy-done.1
  35.0 6.9 %all-to-all-start.1 = ((bf16[16,8,64,128]{3,2,1,0:T(8,128)(2,1)}), bf16[16,8,64,128]{3,2,1,0:T(8,128)(2,1)S(1)}, u32[]{:S(2)}, u32[]{:S(2)}) async-start(bf16[16,8,64,128]{3,2,1,0:T(8,128)(2,1)} %bitcast.107), calls=%async_computation.1 | async-start | bytes 4194304 | tf_op jit(solution)/shard_map/all_to_all | solution.py:55
  42.0 1.1 copy.60
  43.1 0.6 broadcast.151
  43.6 0.7 reduce.16
  44.4 40.2 %all-to-all-done.1 = bf16[16,8,64,128]{3,2,1,0:T(8,128)(2,1)S(1)} async-done(((bf16[16,8,64,128]{3,2,1,0:T(8,128)(2,1)}), bf16[16,8,64,128]{3,2,1,0:T(8,128)(2,1)S(1)}, u32[]{:S(2)}, u32[]{:S(2)}) %all-to-all-start.1) | async-done | bytes 2097184 | tf_op jit(solution)/shard_map/all_to_all | solution.py:55
  84.6 24.0 %while.26 = (s32[]{:T(128)}, f32[256,256]{1,0:T(8,128)}, bf16[2,64,256,128]{3,2,1,0:T(8,128)(2,1)}, s32[2,64]{1,0:T(2,128)S(1)}, bf16[8,64,256]{2,0,1:T(8,128)(2...) while((s32[]{:T(128)}, f32[256,256]{1,0:T(8,128)}, ...), condition=%wide.region_4.5_spmd.clone, body=%wide.region_3.4_spmd.clone.sunk | while | flops 1362231808 | bytes 18614116 | solution.py:81
  84.6 0.7 convolution_convert_fusion.4
  85.4 5.7 %bitcast_dynamic-update-slice_fusion.8 = (bf16[2,64,256,128]{3,2,1,0:T(8,128)(2,1)}, bf16[64,256,128]{2,1,0:T(8,128)(2,1)}) fusion(bf16[2,64,256,128]{3,2,1,0:T(8,128)(2,1)} %get-tuple-element.287, s32[]{:T(128)} %get-tuple-element.285, bf16[2,64,64,128]{3,2,1,0:T(8,128)(2,1)S(1)} %get-tuple-element.298, ...), kind=kOutput, calls=%fused_computation.11.clone.1 | convolution fusion | flops 270532608 | bytes 11535360 | tf_op jit(solution)/shard_map/while/body/eval_jaxpr/sik,sim->skm/dot_general | solution.py:75
  91.1 5.5 %fusion.62 = f32[256,256]{1,0:T(8,128)} fusion(bf16[64,256,128]{2,1,0:T(8,128)(2,1)} %get-tuple-element.275, f32[256,256]{1,0:T(8,128)} %get-tuple-element.286, pred[]{:T(512)S(6)} %compare.26), kind=kOutput, calls=%fused_computation.16.clone.1 | convolution fusion | flops 1073872896 | bytes 4718593 | tf_op jit(solution)/shard_map/while/body/eval_jaxpr/skm,slm->kl/dot_general | solution.py:78
  96.6 0.8 convolution_convert_fusion.4
  97.3 5.8 %bitcast_dynamic-update-slice_fusion.8 = (bf16[2,64,256,128]{3,2,1,0:T(8,128)(2,1)}, bf16[64,256,128]{2,1,0:T(8,128)(2,1)}) fusion(bf16[2,64,256,128]{3,2,1,0:T(8,128)(2,1)} %get-tuple-element.287, s32[]{:T(128)} %get-tuple-element.285, bf16[2,64,64,128]{3,2,1,0:T(8,128)(2,1)S(1)} %get-tuple-element.298, ...), kind=kOutput, calls=%fused_computation.11.clone.1 | convolution fusion | flops 270532608 | bytes 11535360 | tf_op jit(solution)/shard_map/while/body/eval_jaxpr/sik,sim->skm/dot_general | solution.py:75
  103.1 5.5 %fusion.62 = f32[256,256]{1,0:T(8,128)} fusion(bf16[64,256,128]{2,1,0:T(8,128)(2,1)} %get-tuple-element.275, f32[256,256]{1,0:T(8,128)} %get-tuple-element.286, pred[]{:T(512)S(6)} %compare.26), kind=kOutput, calls=%fused_computation.16.clone.1 | convolution fusion | flops 1073872896 | bytes 4718593 | tf_op jit(solution)/shard_map/while/body/eval_jaxpr/skm,slm->kl/dot_general | solution.py:78
  108.6 1.8 copy.61
  110.5 22.5 %all-reduce.3.cloned.1.call-done = f32[256,256]{0,1:T(8,128)} async-done(((f32[256,256]{0,1:T(8,128)}), f32[256,256]{0,1:T(8,128)}) %all-reduce.3.cloned.1.call-update) | async-done | bytes 262160 | tf_op jit(solution)/shard_map/psum | solution.py:84
  133.0 1.0 multiply_add_fusion
  134.1 1.0 fusion.19
  135.2 11.7 %cholesky.49 = f32[128,128]{1,0:T(8,128)S(1)} custom-call(f32[128,128]{1,0:T(8,128)S(1)} %cholesky.115), custom_call_target="Cholesky" | custom-call | tf_op jit(solution)/shard_map/jit(cholesky)/cholesky | solution.py:86
  146.9 9.8 %custom-call.14 = f32[1,128,128]{1,2,0:T(8,128)S(1)} custom-call(f32[1,128,128]{2,1,0:T(8,128)S(1)} %get-tuple-element.177), custom_call_target="InvertDiagBlocksLowerTriangular" | custom-call | tf_op jit(solution)/shard_map/jit(cholesky)/cholesky | solution.py:86
  157.2 11.7 %cholesky.103 = f32[128,128]{1,0:T(8,128)S(1)} custom-call(f32[128,128]{1,0:T(8,128)S(1)} %convolution_subtract_fusion.1), custom_call_target="Cholesky" | custom-call | tf_op jit(solution)/shard_map/jit(cholesky)/cholesky | solution.py:86
  169.3 0.7 compare_reduce_fusion
  171.3 4.0 %while.25 = (s32[]{:T(128)}, f32[256,256]{0,1:T(8,128)S(1)}, s32[2,2]{1,0:T(2,128)S(1)}, f32[2,128,128]{2,1,0:T(8,128)S(1)}, s32[]{:T(128)}) while((s32[]{:T(128)}, f32[256,256]{0,1:T(8,128)S(1)}, s32[2,2]{1,0:T(2,128)S(1)}, f32[2,128,128]{2,1,0:T(8,128)S(1)}, s32[]{:T(128)}) %tuple.70), condition=%wide.while_cond, body=%wide.while_body.sunk | while | flops 2 | bytes 393321 | solution.py:88
  171.3 0.6 fusion.56
  171.8 1.3 dynamic-slice.7
  173.3 0.6 fusion.56
  173.8 1.3 dynamic-slice.7
  175.3 19.9 %custom-call.15 = f32[2,128,128]{1,2,0:T(8,128)S(1)} custom-call(f32[2,128,128]{2,1,0:T(8,128)S(1)} %get-tuple-element.70), custom_call_target="InvertDiagBlocksLowerTriangular" | custom-call | tf_op jit(solution)/shard_map/triangular_solve | solution.py:88
  195.4 0.4 convolution_subtract_fusion
  195.8 0.3 convolution_convert_fusion.2
  196.2 10.5 %while.24 = (s32[]{:T(128)}, f32[2,64,128]{2,1,0:T(8,128)}, bf16[2,64,256,128]{3,2,1,0:T(8,128)(2,1)}, bf16[256,256]{1,0:T(8,128)(2,1)S(1)}, s32[]{:T(128)}) while((s32[]{:T(128)}, f32[2,64,128]{2,1,0:T(8,128)}, bf16[2,64,256,128]{3,2,1,0:T(8,128)(2,1)}, bf16[256,256]{1,0:T(8,128)(2,1)S(1)}, s32[]{:T(128)}) %tuple.73), condition=%wide.region_12.13_spmd, body=%wide.region_10.12_spmd.sunk | while | flops 1077936128 | bytes 4424765 | solution.py:96
  196.2 4.6 %multiply_reduce_fusion.2 = f32[64,128]{1,0:T(8,128)S(1)} fusion(bf16[2,64,256,128]{3,2,1,0:T(8,128)(2,1)} %get-tuple-element.328, s32[]{:T(128)} %get-tuple-element.321, bf16[256,256]{1,0:T(8,128)(2,1)S(1)} %get-tuple-element.329), kind=kOutput, calls=%fused_computation.3.clone.1 | convolution fusion | flops 1077927936 | bytes 4358656 | tf_op jit(solution)/shard_map/while/body/eval_jaxpr/kl,slm->skm/dot_general | solution.py:93
  200.8 0.6 bitcast_dynamic-update-slice_fusion.6
  201.4 4.6 %multiply_reduce_fusion.2 = f32[64,128]{1,0:T(8,128)S(1)} fusion(bf16[2,64,256,128]{3,2,1,0:T(8,128)(2,1)} %get-tuple-element.328, s32[]{:T(128)} %get-tuple-element.321, bf16[256,256]{1,0:T(8,128)(2,1)S(1)} %get-tuple-element.329), kind=kOutput, calls=%fused_computation.3.clone.1 | convolution fusion | flops 1077927936 | bytes 4358656 | tf_op jit(solution)/shard_map/while/body/eval_jaxpr/kl,slm->skm/dot_general | solution.py:93
  206.0 0.6 bitcast_dynamic-update-slice_fusion.6
  206.6 6.8 %all-to-all-start.2 = ((f32[16,8,128]{2,1,0:T(8,128)}), f32[16,8,128]{2,1,0:T(8,128)S(1)}, u32[]{:S(2)}, u32[]{:S(2)}) async-start(f32[16,8,128]{2,1,0:T(8,128)} %bitcast.21), calls=%async_computation.2 | async-start | bytes 131072 | tf_op jit(solution)/shard_map/all_to_all | solution.py:97
  213.5 7.5 %all-to-all-done.2 = f32[16,8,128]{2,1,0:T(8,128)S(1)} async-done(((f32[16,8,128]{2,1,0:T(8,128)}), f32[16,8,128]{2,1,0:T(8,128)S(1)}, u32[]{:S(2)}, u32[]{:S(2)}) %all-to-all-start.2) | async-done | bytes 65568 | tf_op jit(solution)/shard_map/all_to_all | solution.py:97
  221.0 1.2 gather_fusion
  (43 shorter events, 1.9 us)
Async XLA Ops:
  6.5 18.6 %copy-start = (bf16[64,64,128]{2,1,0:T(8,128)(2,1)S(1)}, bf16[64,64,128]{2,1,0:T(8,128)(2,1)}, u32[]{:S(2)}) copy-start(bf16[64,64,128]{2,1,0:T(8,128)(2,1)} %param.12) | copy-start | bytes 3145732
  9.7 23.8 %all-to-all-start = ((s32[16,1,8]{2,1,0:T(1,128)}), s32[16,1,8]{2,1,0:T(1,128)S(1)}, u32[]{:S(2)}, u32[]{:S(2)}) async-start(s32[16,1,8]{2,1,0:T(1,128)} %bitcast.6), calls=%async_computation | async-start | bytes 16384 | tf_op jit(solution)/shard_map/all_to_all | solution.py:56
  24.5 0.7 copy-start.2
  33.6 1.4 copy-start.1
  35.0 49.6 %all-to-all-start.1 = ((bf16[16,8,64,128]{3,2,1,0:T(8,128)(2,1)}), bf16[16,8,64,128]{3,2,1,0:T(8,128)(2,1)S(1)}, u32[]{:S(2)}, u32[]{:S(2)}) async-start(bf16[16,8,64,128]{3,2,1,0:T(8,128)(2,1)} %bitcast.107), calls=%async_computation.1 | async-start | bytes 4194304 | tf_op jit(solution)/shard_map/all_to_all | solution.py:55
  41.9 91.1 %all-reduce.3.cloned.1.call-start = ((), (), s32[]{:S(2)}) async-start(), calls=%async_computation.3 | async-start | bytes 524288 | tf_op jit(solution)/shard_map/psum | solution.py:84
  84.6 48.4 %copy-start.3 = (f32[1,256]{1,0:T(1,128)S(1)}, f32[1,256]{1,0:T(1,128)}, u32[]{:S(2)}) copy-start(f32[1,256]{1,0:T(1,128)} %param.19) | copy-start | bytes 3076
  206.6 14.4 %all-to-all-start.2 = ((f32[16,8,128]{2,1,0:T(8,128)}), f32[16,8,128]{2,1,0:T(8,128)S(1)}, u32[]{:S(2)}, u32[]{:S(2)}) async-start(f32[16,8,128]{2,1,0:T(8,128)} %bitcast.21), calls=%async_computation.2 | async-start | bytes 131072 | tf_op jit(solution)/shard_map/all_to_all | solution.py:97
Sparse Core Ops, SparseCore 0:
  110.5 22.4 all-reduce.2
where the time goes:
time: 230 us; the launch traced here: 229 us
  waiting for transfers between devices  70.3 us (31%)
  other arithmetic  59.4 us (26%)
  matrix products  41.9 us (18%)
  starting transfers between devices  22.1 us (10%)
  local copies, waits for them, and re-layouts  20.3 us (9%)
  between operations  14.9 us (6%)
    all_to_all x1, waiting for transfers between devices, per_device(): lax.all_to_all(record_send, 'sub', split_axis=0, concat_axis=0, tiled=True)  40.2 us
    another operation x6, other arithmetic, per_device(): factor = jnp.linalg.cholesky(pencil)  34 us
    psum x1, waiting for transfers between devices, per_device(): gram_sum = lax.psum(gram_sum, 'mode')  22.5 us
    another operation x4, other arithmetic, per_device(): lax.linalg.triangular_solve(factor, identity, left_side=True, lower=True)  19.9 us
    dot_general x2, matrix products, project(): jnp.einsum('sik,sim->skm', parent_rows, record_part, preferred_element_ty...  11.5 us
    dot_general x2, matrix products, project(): jnp.einsum('skm,slm->kl', projected, projected, preferred_element_type=jn...  11 us
    dot_general x2, matrix products, strength(): jnp.einsum('kl,slm->skm', inverse, projected, preferred_element_type=jnp....  9.22 us
    all_to_all x1, starting transfers between devices, per_device(): lax.all_to_all(row_send, 'sub', split_axis=0, concat_axis=0, tiled=True)  8.34 us
  transfers between devices with their start and end apart: 4, of which 3 were waited for; matrix products, arithmetic and copies ran while one was open for 8% of the time, Pallas kernels for 0%

commit v1 on v0

v1 whole, which is shorter than its diff:
```python
import functools

import jax
import jax.numpy as jnp
from jax import lax
from jax.experimental import pallas as pl
from jax.experimental.pallas import tpu as pltpu
from jax.sharding import PartitionSpec as P

MESH = pl.DeviceIdType.MESH
F32 = jnp.float32
BF16 = jnp.bfloat16
HALVES = 2


def dot(a, b, dims=((1,), (0,)), precision=None):
    return lax.dot_general(a, b, (dims, ((), ())), preferred_element_type=F32, precision=precision)


def exact(a, b, dims=((1,), (0,))):
    return dot(a, b, dims, lax.Precision.HIGHEST)


def split(x, terms):
    parts = []
    for _ in range(terms):
        part = x.astype(BF16)
        parts.append(part)
        x = x - part.astype(F32)
    return parts


def placed(record, right):
    zero = jnp.zeros_like(record)
    return jnp.concatenate(
        [jnp.where(right == 0, record, zero), jnp.where(right == 0, zero, record)], axis=0
    )


def record_kernel(
    children, group, parents, pair_ref, owner_ref, row_ref, coupling_ref, modes_ref, weight_ref, record_ref, gram_ref
):
    step = pl.program_id(0)

    @pl.when(step == 0)
    def _():
        @pl.loop(0, gram_ref.shape[0])
        def _(i):
            gram_ref[i] = jnp.zeros(gram_ref.shape[1:], F32)

    for i in range(group):
        child = step * group + i
        picked = jnp.concatenate(
            [modes_ref[i, pair_ref[child, k]] for k in range(pair_ref.shape[1])], axis=0
        )
        record = dot(coupling_ref[i], picked) * weight_ref[pl.ds(i, 1), :].astype(F32)
        record = record.astype(BF16)
        record_ref[i] = record
        block = row_ref[child]
        slot = ((block // 4) * 2 + (block // 2) % 2) * parents + owner_ref[child, 0]
        gram_ref[slot] += dot(record, placed(record, block % 2), ((1,), (1,)))


def records_and_grams(coupling, pairs, modes, weights, owner, row_block, parents):
    children, block, width = coupling.shape
    columns = modes.shape[2]
    blocks = modes.shape[1] // block
    group = 8
    return pl.pallas_call(
        functools.partial(record_kernel, children, group, parents),
        grid_spec=pltpu.PrefetchScalarGridSpec(
            num_scalar_prefetch=3,
            grid=(children // group,),
            in_specs=[
                pl.BlockSpec((group, block, width), lambda i, *_: (i, 0, 0)),
                pl.BlockSpec((group, blocks, block, columns), lambda i, *_: (i, 0, 0, 0)),
                pl.BlockSpec((group, columns), lambda i, *_: (i, 0)),
            ],
            out_specs=[
                pl.BlockSpec((group, block, columns), lambda i, *_: (i, 0, 0)),
                pl.BlockSpec((4 * parents, block, 2 * block), lambda i, *_: (0, 0, 0)),
            ],
        ),
        out_shape=[
            jax.ShapeDtypeStruct((children, block, columns), BF16),
            jax.ShapeDtypeStruct((4 * parents, block, 2 * block), F32),
        ],
        name="records",
    )(pairs, owner, row_block, coupling, modes.reshape(children, blocks, block, columns), weights)


def invert_block(matrix):
    size = matrix.shape[0]
    rows = 8
    lane = lax.broadcasted_iota(jnp.int32, (rows, size), 1)
    row = lax.broadcasted_iota(jnp.int32, (rows, size), 0)

    def turn(_, tiles):
        tiles = list(tiles)
        for j in range(rows):
            at_lane = lane == j
            pivot_row = jnp.broadcast_to(tiles[0][j : j + 1, :], (rows, size))
            scale = 1.0 / jnp.broadcast_to(tiles[0][j : j + 1, j : j + 1], (rows, size))
            scaled = jnp.where(at_lane, scale, pivot_row * scale)
            for t in range(len(tiles)):
                column = jnp.broadcast_to(tiles[t][:, j : j + 1], (rows, size))
                tiles[t] = jnp.where(at_lane, 0.0, tiles[t]) - column * scaled
            tiles[0] = jnp.where(row == j, scaled, tiles[0])
        tiles = tiles[1:] + tiles[:1]
        return tuple(pltpu.roll(t, size - rows, 1) for t in tiles)

    tiles = tuple(matrix[i * rows : (i + 1) * rows, :] for i in range(size // rows))
    tiles = lax.fori_loop(0, size // rows, turn, tiles)
    return jnp.concatenate(tiles, axis=0)


def exchange_kernel(
    subs, scale, owner_ref, row_ref, gram_ref, record_ref, parent_ref, eig_ref,
    out_ref,
    factor_ref, work,
    sib, recv_a, recv_b, recv_c, tile, tile_sib, spread, send_sem, recv_sem,
):
    zs = subs // 4
    me = lax.axis_index("sub")
    core = lax.axis_index("mode")
    z, y, x = me // 4, (me // 2) % 2, me % 2

    def place(zz, yy, xx):
        return ((zz * 2 + yy) * 2 + xx, core)

    sibling = (me, 1 - core)
    near_x, near_y = place(z, y, 1 - x), place(z, 1 - y, x)
    far = [place((z + d) % zs, y, x) for d in range(1, zs)]

    barrier = pltpu.get_barrier_semaphore()
    for peer in [sibling, near_x, near_y] + far:
        pl.semaphore_signal(barrier, inc=1, device_id=peer, device_id_type=MESH)
    pl.semaphore_wait(barrier, 3 + len(far))

    count = [0]

    def send(src, dst, peer):
        k = count[0]
        count[0] += 1
        copy = pltpu.make_async_remote_copy(
            src_ref=src, dst_ref=dst, send_sem=send_sem.at[k], recv_sem=recv_sem.at[k],
            device_id=peer, device_id_type=MESH,
        )
        copy.start()
        return copy

    copies = [send(gram_ref.at[1 - core, k], sib.at[k], sibling) for k in range(HALVES)]
    first = []
    for k in range(HALVES):
        copies[k].wait()

        @pl.loop(0, zs)
        def _(zz, k=k):
            for yy in range(2):
                for xx in range(2):
                    sib[k, zz, yy, xx] += gram_ref[core, k, zz, yy, xx]

        if k == 0:
            first.append(send(sib.at[0, :, :, 1 - x], recv_a.at[0], near_x))
        else:
            first.append(send(sib.at[1, :, 1 - y], recv_a.at[1], near_y))
    second = []
    for k in range(HALVES):
        first[k].wait()

        @pl.loop(0, zs)
        def _(zz, k=k):
            for i in range(2):
                mine = sib[0, zz, i, x] if k == 0 else sib[1, zz, y, i]
                recv_a[k, zz, i] += mine

        if k == 0:
            second.append(send(recv_a.at[0, :, 1 - y], recv_b.at[0], near_y))
        else:
            second.append(send(recv_a.at[1, :, 1 - x], recv_b.at[1], near_x))
    for k in range(HALVES):
        second[k].wait()

        @pl.loop(0, zs)
        def _(zz, k=k):
            recv_b[k, zz] += recv_a[k, zz, y if k == 0 else x]

    third = []
    for d in range(1, zs):
        there = (z + d) % zs
        third.append(send(recv_b.at[:, there], recv_c.at[d - 1], far[d - 1]))
    total = recv_b[:, z]
    for d in range(1, zs):
        third[d - 1].wait()
        total = total + recv_c[d - 1]
    tile[core] = total
    pair = send(tile.at[core], tile.at[core], sibling)
    pair.wait()

    size = parent_ref.shape[1]
    block = tile.shape[2]
    for h in range(2):
        for k in range(HALVES):
            both = split(tile[h, k], 3)
            for r in range(2):
                b = (h * 2 + k) * 2 + r
                rows = parent_ref[b * block : (b + 1) * block, :]
                part = sum(dot(t[:, r * block : (r + 1) * block], rows) for t in both)
                factor_ref[b * block : (b + 1) * block, :] = part
    total = jnp.zeros((size, size), F32)
    for part in split(factor_ref[...], 3):
        total = total + dot(parent_ref[...], part, ((0,), (0,)))
    diagonal = lax.broadcasted_iota(jnp.int32, (size, size), 0) == lax.broadcasted_iota(
        jnp.int32, (size, size), 1
    )
    work[...] = jnp.where(diagonal, eig_ref[...], 0.0) + total * scale

    half = size // 2
    top = invert_block(work[:half, :half])
    cross = work[:half, half:]
    ratio = exact(top, cross)
    corner = invert_block(work[half:, half:] - exact(cross, ratio, ((0,), (0,))))
    side = exact(ratio, corner)
    work[half:, half:] = corner
    work[:half, half:] = -side
    work[half:, :half] = -side.T
    work[:half, :half] = top + exact(side, ratio, ((1,), (1,)))

    span = 2 * HALVES * block
    mine = parent_ref[pl.ds(pl.multiple_of(core * span, span), span), :]
    turned = sum(dot(mine, part) for part in split(work[...], 3))
    factor_ref[:span, :] = turned
    for k in range(HALVES):
        for r in range(2):
            at = (k * 2 + r) * block
            rows = factor_ref[at : at + block, :]
            base = parent_ref[pl.ds(pl.multiple_of(core * span + at, block), block), :]
            value = sum(dot(part, base, ((1,), (1,))) for part in split(rows, 2))
            for t, part in enumerate(split(value, 2)):
                tile_sib[k, t, :, r * block : (r + 1) * block] = part

    for k in range(HALVES):
        for t in range(2):
            spread[core, k, z, y, x, t] = tile_sib[k, t]
    own = [send(spread.at[core, :, z, y, x], spread.at[core, :, z, y, x], peer) for peer in far]
    for copy in own:
        copy.wait()
    a = spread.at[core, 0, :, y, x]
    b = spread.at[core, 1, :, y, x]
    up = [send(a, a, near_y), send(b, b, near_x)]
    for copy in up:
        copy.wait()
    a = spread.at[core, 0, :, :, x]
    b = spread.at[core, 1, :, y]
    last = [send(a, a, near_x), send(b, b, near_y)]
    across = [
        send(spread.at[core, 0, :, :, x], spread.at[core, 0, :, :, x], sibling),
        send(spread.at[core, 1, :, y], spread.at[core, 1, :, y], sibling),
    ]
    for copy in last:
        copy.wait()
    across.append(send(spread.at[core, 0, :, :, 1 - x], spread.at[core, 0, :, :, 1 - x], sibling))
    across.append(send(spread.at[core, 1, :, 1 - y], spread.at[core, 1, :, 1 - y], sibling))
    for copy in across:
        copy.wait()

    group = 8

    @pl.loop(0, record_ref.shape[0] // group)
    def _(step):
        values = []
        for i in range(group):
            child = step * group + i
            record = record_ref[child]
            parent, row = owner_ref[child, 0], row_ref[child]
            form = spread[row // 4, (row // 2) % 2, parent // 4, (parent // 2) % 2, parent % 2]
            pushed = dot(form.reshape(2 * block, 2 * block), placed(record, row % 2))
            pushed = pushed[:block] + pushed[block:]
            values.append(jnp.sum(record.astype(F32) * pushed, axis=0, keepdims=True))
        out_ref[pl.ds(pl.multiple_of(step * group, group), group), :] = (
            jnp.concatenate(values, axis=0) / size
        )


def strengths(owner, row_block, grams, records, parent, eigs, subs, scale):
    children, block, columns = records.shape
    rows, size = parent.shape
    zs = subs // 4
    tile = (block, 2 * block)
    copies = 16 + 2 * (zs - 1)
    vmem = pl.BlockSpec(memory_space=pltpu.VMEM)
    smem = pl.BlockSpec(memory_space=pltpu.SMEM)
    return pl.pallas_call(
        functools.partial(exchange_kernel, subs, scale),
        in_specs=[smem, smem, vmem, vmem, vmem, vmem],
        out_specs=vmem,
        out_shape=jax.ShapeDtypeStruct((children, columns), F32),
        scratch_shapes=[
            pltpu.VMEM((rows, size), F32),
            pltpu.VMEM((size, size), F32),
            pltpu.VMEM((HALVES, zs, 2, 2) + tile, F32),
            pltpu.VMEM((HALVES, zs, 2) + tile, F32),
            pltpu.VMEM((HALVES, zs) + tile, F32),
            pltpu.VMEM((max(1, zs - 1), HALVES) + tile, F32),
            pltpu.VMEM((2, HALVES) + tile, F32),
            pltpu.VMEM((HALVES, 2) + tile, BF16),
            pltpu.VMEM((2, HALVES, zs, 2, 2, 2) + tile, BF16),
            pltpu.SemaphoreType.DMA((copies,)),
            pltpu.SemaphoreType.DMA((copies,)),
        ],
        compiler_params=pltpu.CompilerParams(
            collective_id=0, has_side_effects=True, vmem_limit_bytes=60 << 20
        ),
        name="exchange",
    )(owner, row_block, grams.reshape((2, HALVES, zs, 2, 2) + tile), records, parent, eigs)


def per_device(
    coupling, coupling_pairs, modes, mode_weights, parent_of, row_block, parent_modes, parent_eigs
):
    subs = lax.axis_size("sub")
    parents = subs * parent_modes.shape[0]
    records, grams = records_and_grams(
        coupling, coupling_pairs, modes, mode_weights, parent_of, row_block, parents
    )
    scale = 1.0 / (coupling.shape[0] * modes.shape[2] * lax.axis_size("mode"))
    return strengths(
        parent_of, row_block, grams, records, parent_modes[0], parent_eigs, subs, scale
    )


def solution(mesh):
    in_specs = (
        P("sub", None, None),
        P("sub", None),
        P("sub", None, "mode"),
        P("sub", "mode"),
        P("sub", None),
        P("sub"),
        P("sub", None, None),
        P("sub", None),
    )
    return jax.shard_map(
        per_device, mesh=mesh, in_specs=in_specs, out_specs=P("sub", "mode"), check_vma=False
    )
```

time: 230 us -> 104 us (0.45)
  Pallas kernels: 0 us -> 98.9 us
  waiting for transfers between devices: 70.3 us -> 0 us
  other arithmetic: 59.4 us -> 0 us
  matrix products: 41.9 us -> 0 us
  starting transfers between devices: 22.1 us -> 0 us
  local copies, waits for them, and re-layouts: 20.3 us -> 4.1 us
  between operations: 14.9 us -> 0.01 us
    pallas_call x0 -> x2, Pallas kernels: none -> 98.9 us  [the longest x1 86.8 us: strengths(): pl.pallas_call(functools.partial(exchange_kernel, subs, scale), in_specs=...]
    another operation x10 -> x0, other arithmetic: 53.9 us -> none  [the longest x6 34 us: per_device(): factor = jnp.linalg.cholesky(pencil)]
    all_to_all x3 -> x0, waiting for transfers between devices: 47.7 us -> none  [the longest x1 40.2 us: per_device(): lax.all_to_all(record_send, 'sub', split_axis=0, concat_axis=0, tiled=True)]
    dot_general x10 -> x0, matrix products: 40.4 us -> none  [the longest x2 11.5 us: project(): jnp.einsum('sik,sim->skm', parent_rows, record_part, preferred_element_ty...]
    psum x1 -> x0, waiting for transfers between devices: 22.5 us -> none  [per_device(): gram_sum = lax.psum(gram_sum, 'mode')]
    all_to_all x3 -> x0, starting transfers between devices: 22.1 us -> none  [the longest x1 8.34 us: per_device(): lax.all_to_all(row_send, 'sub', split_axis=0, concat_axis=0, tiled=True)]
    scatter x2 -> x0, local copies, waits for them, and re-layouts: 7.09 us -> none  [to_slots(): return empty.at[slot_index].set(values)]
    another operation x19 -> x0, local copies, waits for them, and re-layouts: 4.37 us -> none
  transfers between devices with their start and end apart: 4 -> 0, of which waited for: 3 -> 0; matrix products, arithmetic and copies ran while one was open for 8% -> 0% of each run, Pallas kernels for 0% -> 0%
where the time goes in v1:
time: 104 us; the launch traced here: 103 us
  Pallas kernels  98.9 us (95%)
  local copies, waits for them, and re-layouts  4.1 us (4%)
    pallas_call x1, Pallas kernels, strengths(): pl.pallas_call(functools.partial(exchange_kernel, subs, scale), in_specs=...  86.8 us
    pallas_call x1, Pallas kernels, records_and_grams(): pl.pallas_call(functools.partial(record_kernel, children, group, parents)...  12.1 us
    unnamed x3, local copies, waits for them, and re-layouts  4.1 us

profile of v1, /device:TPU:0, one launch (start us, length us, event | category | flops | bytes accessed | tf_op | source)
XLA Modules:
  0.0 103.0 jit_solution(14691428318837905954)
XLA Ops:
  0.0 1.4 %copy.11.owner_ref = s32[64,1]{1,0:T(8,128)} copy(s32[64,1]{0,1:T(1,128)} %param.12) | data formatting | bytes 512 | tf_op args[4]
  1.4 1.4 %copy.9.pair_ref = s32[64,2]{1,0:T(8,128)} copy(s32[64,2]{0,1:T(2,128)} %param.9) | data formatting | bytes 1024 | tf_op args[1]
  2.7 12.1 %records.1 = (bf16[64,64,128]{2,1,0:T(8,128)(2,1)}, f32[64,64,128]{2,1,0:T(8,128)}) custom-call(s32[64,2]{1,0:T(8,128)} %copy.9.pair_ref, s32[64,1]{1,0:T(8,128)} %copy.11.owner_ref, s32[64]{0:T(128)} %row_ref.3, bf16[64,64,128]{2,1,0:T(8,128)(2,1)} %coupling_ref.1, bf16[64,4,64,128]{3,2,1,0:T(8,128)(2,1)} %bitcast.3, bf16[64,128]{1,0:T(8,128)(2,1)} %weight_ref.1), custom_call_target="tpu_custom_call" | custom-call | tf_op jit(solution)/shard_map/records/pallas_call | solution.py:69
  14.8 86.8 %exchange.1 = f32[64,128]{1,0:T(8,128)} custom-call(s32[64,1]{1,0:T(8,128)} %copy.11.owner_ref, s32[64]{0:T(128)} %row_ref.3, f32[2,2,4,2,2,64,128]{6,5,4,3,2,1,0:T(8,128)} %bitcast.4, bf16[64,64,128]{2,1,0:T(8,128)(2,1)} %get-tuple-element.8.record_ref, bf16[512,256]{1,0:T(8,128)(2,1)} %bitcast.5, f32[1,256]{1,0:T(1,128)} %eig_ref.1), custom_call_target="tpu_custom_call" | custom-call | tf_op jit(solution)/shard_map/exchange/pallas_call | solution.py:293
  101.6 1.4 %copy.13 = f32[64,128]{1,0:T(8,128)} copy(f32[64,128]{1,0:T(8,128)} %exchange.1) | data formatting | bytes 65536

commit v2 on v1

--- a/solution.py
+++ b/solution.py
@@ -97,15 +97,29 @@
 
     def turn(_, tiles):
         tiles = list(tiles)
-        for j in range(rows):
-            at_lane = lane == j
-            pivot_row = jnp.broadcast_to(tiles[0][j : j + 1, :], (rows, size))
-            scale = 1.0 / jnp.broadcast_to(tiles[0][j : j + 1, j : j + 1], (rows, size))
-            scaled = jnp.where(at_lane, scale, pivot_row * scale)
+        for j in range(0, rows, 2):
+            first, second = lane == j, lane == j + 1
+            pair = jnp.logical_or(first, second)
+
+            def spread_row(i):
+                return jnp.broadcast_to(tiles[0][i : i + 1, :], (rows, size))
+
+            def spread_at(i, k):
+                return jnp.broadcast_to(tiles[0][i : i + 1, k : k + 1], (rows, size))
+
+            p, q = spread_row(j), spread_row(j + 1)
+            a, b, c, d = (
+                spread_at(j, j), spread_at(j, j + 1), spread_at(j + 1, j), spread_at(j + 1, j + 1)
+            )
+            scale = 1.0 / (a * d - b * c)
+            a, b, c, d = a * scale, b * scale, c * scale, d * scale
+            u = jnp.where(first, d, jnp.where(second, -b, d * p - b * q))
+            v = jnp.where(first, -c, jnp.where(second, a, a * q - c * p))
             for t in range(len(tiles)):
-                column = jnp.broadcast_to(tiles[t][:, j : j + 1], (rows, size))
-                tiles[t] = jnp.where(at_lane, 0.0, tiles[t]) - column * scaled
-            tiles[0] = jnp.where(row == j, scaled, tiles[0])
+                left = jnp.broadcast_to(tiles[t][:, j : j + 1], (rows, size))
+                right = jnp.broadcast_to(tiles[t][:, j + 1 : j + 2], (rows, size))
+                tiles[t] = jnp.where(pair, 0.0, tiles[t]) - left * u - right * v
+            tiles[0] = jnp.where(row == j, u, jnp.where(row == j + 1, v, tiles[0]))
         tiles = tiles[1:] + tiles[:1]
         return tuple(pltpu.roll(t, size - rows, 1) for t in tiles)
 
@@ -236,12 +250,10 @@
             rows = factor_ref[at : at + block, :]
             base = parent_ref[pl.ds(pl.multiple_of(core * span + at, block), block), :]
             value = sum(dot(part, base, ((1,), (1,))) for part in split(rows, 2))
-            for t, part in enumerate(split(value, 2)):
-                tile_sib[k, t, :, r * block : (r + 1) * block] = part
-
-    for k in range(HALVES):
-        for t in range(2):
-            spread[core, k, z, y, x, t] = tile_sib[k, t]
+            tile_sib[k, :, r * block : (r + 1) * block] = value.astype(BF16)
+
+    for k in range(HALVES):
+        spread[core, k, z, y, x] = tile_sib[k]
     own = [send(spread.at[core, :, z, y, x], spread.at[core, :, z, y, x], peer) for peer in far]
     for copy in own:
         copy.wait()
@@ -274,8 +286,7 @@
             record = record_ref[child]
             parent, row = owner_ref[child, 0], row_ref[child]
             form = spread[row // 4, (row // 2) % 2, parent // 4, (parent // 2) % 2, parent % 2]
-            pushed = dot(form.reshape(2 * block, 2 * block), placed(record, row % 2))
-            pushed = pushed[:block] + pushed[block:]
+            pushed = dot(form, placed(record, row % 2))
             values.append(jnp.sum(record.astype(F32) * pushed, axis=0, keepdims=True))
         out_ref[pl.ds(pl.multiple_of(step * group, group), group), :] = (
             jnp.concatenate(values, axis=0) / size
@@ -303,8 +314,8 @@
             pltpu.VMEM((HALVES, zs) + tile, F32),
             pltpu.VMEM((max(1, zs - 1), HALVES) + tile, F32),
             pltpu.VMEM((2, HALVES) + tile, F32),
-            pltpu.VMEM((HALVES, 2) + tile, BF16),
-            pltpu.VMEM((2, HALVES, zs, 2, 2, 2) + tile, BF16),
+            pltpu.VMEM((HALVES,) + tile, BF16),
+            pltpu.VMEM((2, HALVES, zs, 2, 2) + tile, BF16),
             pltpu.SemaphoreType.DMA((copies,)),
             pltpu.SemaphoreType.DMA((copies,)),
         ],

time: 104 us -> 85.1 us (0.82)
  Pallas kernels: 98.9 us -> 80.5 us
    pallas_call x1, Pallas kernels: 86.8 us -> 68.4 us  [strengths(): pl.pallas_call(functools.partial(exchange_kernel, subs, scale), in_specs=...]
where the time goes in v2:
time: 85.1 us; the launch traced here: 84.6 us
  Pallas kernels  80.5 us (95%)
  local copies, waits for them, and re-layouts  4.1 us (5%)
    pallas_call x1, Pallas kernels, strengths(): pl.pallas_call(functools.partial(exchange_kernel, subs, scale), in_specs=...  68.4 us
    pallas_call x1, Pallas kernels, records_and_grams(): pl.pallas_call(functools.partial(record_kernel, children, group, parents)...  12.1 us
    unnamed x3, local copies, waits for them, and re-layouts  4.1 us

profile of v2, /device:TPU:0, one launch (start us, length us, event | category | flops | bytes accessed | tf_op | source)
XLA Modules:
  0.0 84.6 jit_solution(3265945883665225706)
XLA Ops:
  0.0 1.4 %copy.11.owner_ref = s32[64,1]{1,0:T(8,128)} copy(s32[64,1]{0,1:T(1,128)} %param.12) | data formatting | bytes 512 | tf_op args[4]
  1.4 1.4 %copy.9.pair_ref = s32[64,2]{1,0:T(8,128)} copy(s32[64,2]{0,1:T(2,128)} %param.9) | data formatting | bytes 1024 | tf_op args[1]
  2.7 12.1 %records.1 = (bf16[64,64,128]{2,1,0:T(8,128)(2,1)}, f32[64,64,128]{2,1,0:T(8,128)}) custom-call(s32[64,2]{1,0:T(8,128)} %copy.9.pair_ref, s32[64,1]{1,0:T(8,128)} %copy.11.owner_ref, s32[64]{0:T(128)} %row_ref.3, bf16[64,64,128]{2,1,0:T(8,128)(2,1)} %coupling_ref.1, bf16[64,4,64,128]{3,2,1,0:T(8,128)(2,1)} %bitcast.3, bf16[64,128]{1,0:T(8,128)(2,1)} %weight_ref.1), custom_call_target="tpu_custom_call" | custom-call | tf_op jit(solution)/shard_map/records/pallas_call | solution.py:69
  14.8 68.4 %exchange.1 = f32[64,128]{1,0:T(8,128)} custom-call(s32[64,1]{1,0:T(8,128)} %copy.11.owner_ref, s32[64]{0:T(128)} %row_ref.3, f32[2,2,4,2,2,64,128]{6,5,4,3,2,1,0:T(8,128)} %bitcast.4, bf16[64,64,128]{2,1,0:T(8,128)(2,1)} %get-tuple-element.8.record_ref, bf16[512,256]{1,0:T(8,128)(2,1)} %bitcast.5, f32[1,256]{1,0:T(1,128)} %eig_ref.1), custom_call_target="tpu_custom_call" | custom-call | tf_op jit(solution)/shard_map/exchange/pallas_call | solution.py:304
  83.2 1.4 %copy.13 = f32[64,128]{1,0:T(8,128)} copy(f32[64,128]{1,0:T(8,128)} %exchange.1) | data formatting | bytes 65536

commit v3 on v2

--- a/solution.py
+++ b/solution.py
@@ -37,8 +37,15 @@
     )
 
 
+def below(block):
+    shape = (block, 2 * block)
+    row = lax.broadcasted_iota(jnp.int32, shape, 0)
+    lane = lax.broadcasted_iota(jnp.int32, shape, 1)
+    return row, jnp.where(lane < block, lane, lane - block)
+
+
 def record_kernel(
-    children, group, parents, pair_ref, owner_ref, row_ref, coupling_ref, modes_ref, weight_ref, record_ref, gram_ref
+    group, parents, index_ref, coupling_ref, modes_ref, weight_ref, record_ref, pack_ref, gram_ref
 ):
     step = pl.program_id(0)
 
@@ -48,28 +55,51 @@
         def _(i):
             gram_ref[i] = jnp.zeros(gram_ref.shape[1:], F32)
 
+    pairs = index_ref.shape[0] - 2
+    products = []
     for i in range(group):
         child = step * group + i
         picked = jnp.concatenate(
-            [modes_ref[i, pair_ref[child, k]] for k in range(pair_ref.shape[1])], axis=0
+            [modes_ref[i, index_ref[2 + k, child]] for k in range(pairs)], axis=0
         )
         record = dot(coupling_ref[i], picked) * weight_ref[pl.ds(i, 1), :].astype(F32)
         record = record.astype(BF16)
         record_ref[i] = record
-        block = row_ref[child]
-        slot = ((block // 4) * 2 + (block // 2) % 2) * parents + owner_ref[child, 0]
-        gram_ref[slot] += dot(record, placed(record, block % 2), ((1,), (1,)))
-
-
-def records_and_grams(coupling, pairs, modes, weights, owner, row_block, parents):
+        side = index_ref[1, child] % 2
+        products.append(dot(record, placed(record, side), ((1,), (1,))))
+    for i in range(group):
+        child = step * group + i
+        gram_ref[(index_ref[1, child] // 2) * parents + index_ref[0, child]] += products[i]
+
+    @pl.when(step == pl.num_programs(0) - 1)
+    def _():
+        block = gram_ref.shape[1]
+        part = block // 2
+        row, column = below(block)
+
+        @pl.loop(0, parents)
+        def _(p):
+            for h in range(2):
+                high, low = h * 2 * parents + p, (h * 2 + 1) * parents + p
+                upper, lower = gram_ref[high], gram_ref[low]
+                packed = jnp.where(row <= column, upper, lower)
+                diagonal = jnp.sum(jnp.where(row == column, lower, 0.0), axis=0, keepdims=True)
+                pack_ref[high, :part] = packed[:part]
+                pack_ref[high, part:] = jnp.broadcast_to(diagonal, (8, 2 * block))
+                pack_ref[low, :part] = packed[part:]
+                pack_ref[low, part:] = jnp.zeros((8, 2 * block), F32)
+
+
+def records_and_grams(index, coupling, modes, weights, parents):
     children, block, width = coupling.shape
     columns = modes.shape[2]
     blocks = modes.shape[1] // block
-    group = 8
+    group = 16
+    packed = (4 * parents, block // 2 + 8, 2 * block)
     return pl.pallas_call(
-        functools.partial(record_kernel, children, group, parents),
+        functools.partial(record_kernel, group, parents),
         grid_spec=pltpu.PrefetchScalarGridSpec(
-            num_scalar_prefetch=3,
+            num_scalar_prefetch=1,
             grid=(children // group,),
             in_specs=[
                 pl.BlockSpec((group, block, width), lambda i, *_: (i, 0, 0)),
@@ -78,15 +108,16 @@
             ],
             out_specs=[
                 pl.BlockSpec((group, block, columns), lambda i, *_: (i, 0, 0)),
-                pl.BlockSpec((4 * parents, block, 2 * block), lambda i, *_: (0, 0, 0)),
+                pl.BlockSpec(packed, lambda i, *_: (0, 0, 0)),
             ],
+            scratch_shapes=[pltpu.VMEM((4 * parents, block, 2 * block), F32)],
         ),
         out_shape=[
             jax.ShapeDtypeStruct((children, block, columns), BF16),
-            jax.ShapeDtypeStruct((4 * parents, block, 2 * block), F32),
+            jax.ShapeDtypeStruct(packed, F32),
         ],
         name="records",
-    )(pairs, owner, row_block, coupling, modes.reshape(children, blocks, block, columns), weights)
+    )(index, coupling, modes.reshape(children, blocks, block, columns), weights)
 
 
 def invert_block(matrix):
@@ -129,7 +160,7 @@
 
 
 def exchange_kernel(
-    subs, scale, owner_ref, row_ref, gram_ref, record_ref, parent_ref, eig_ref,
+    subs, scale, index_ref, gram_ref, record_ref, parent_ref, eig_ref,
     out_ref,
     factor_ref, work,
     sib, recv_a, recv_b, recv_c, tile, tile_sib, spread, send_sem, recv_sem,
@@ -212,22 +243,30 @@
     pair.wait()
 
     size = parent_ref.shape[1]
-    block = tile.shape[2]
+    block = spread.shape[-2]
+    part = block // 2
+    row, column = below(block)
     for h in range(2):
+        packed = jnp.concatenate([tile[h, 0, :part], tile[h, 1, :part]], axis=0)
+        lower_diagonal = jnp.broadcast_to(tile[h, 0, part : part + 1], packed.shape)
         for k in range(HALVES):
-            both = split(tile[h, k], 3)
+            inside = row < column if k == 0 else row > column
+            middle = packed if k == 0 else lower_diagonal
+            triangle = jnp.where(inside, packed, jnp.where(row == column, 0.5 * middle, 0.0))
+            terms = split(triangle, 3)
             for r in range(2):
                 b = (h * 2 + k) * 2 + r
                 rows = parent_ref[b * block : (b + 1) * block, :]
-                part = sum(dot(t[:, r * block : (r + 1) * block], rows) for t in both)
-                factor_ref[b * block : (b + 1) * block, :] = part
+                factor_ref[b * block : (b + 1) * block, :] = sum(
+                    dot(t[:, r * block : (r + 1) * block], rows) for t in terms
+                )
     total = jnp.zeros((size, size), F32)
-    for part in split(factor_ref[...], 3):
-        total = total + dot(parent_ref[...], part, ((0,), (0,)))
+    for term in split(factor_ref[...], 3):
+        total = total + dot(parent_ref[...], term, ((0,), (0,)))
     diagonal = lax.broadcasted_iota(jnp.int32, (size, size), 0) == lax.broadcasted_iota(
         jnp.int32, (size, size), 1
     )
-    work[...] = jnp.where(diagonal, eig_ref[...], 0.0) + total * scale
+    work[...] = jnp.where(diagonal, eig_ref[...], 0.0) + (total + total.T) * scale
 
     half = size // 2
     top = invert_block(work[:half, :half])
@@ -284,36 +323,37 @@
         for i in range(group):
             child = step * group + i
             record = record_ref[child]
-            parent, row = owner_ref[child, 0], row_ref[child]
-            form = spread[row // 4, (row // 2) % 2, parent // 4, (parent // 2) % 2, parent % 2]
-            pushed = dot(form, placed(record, row % 2))
+            parent, place_row = index_ref[0, child], index_ref[1, child]
+            form = spread[place_row // 4, (place_row // 2) % 2, parent // 4, (parent // 2) % 2, parent % 2]
+            pushed = dot(form, placed(record, place_row % 2))
             values.append(jnp.sum(record.astype(F32) * pushed, axis=0, keepdims=True))
         out_ref[pl.ds(pl.multiple_of(step * group, group), group), :] = (
             jnp.concatenate(values, axis=0) / size
         )
 
 
-def strengths(owner, row_block, grams, records, parent, eigs, subs, scale):
+def strengths(index, grams, records, parent, eigs, subs, scale):
     children, block, columns = records.shape
     rows, size = parent.shape
     zs = subs // 4
     tile = (block, 2 * block)
+    packed = grams.shape[1:]
     copies = 16 + 2 * (zs - 1)
     vmem = pl.BlockSpec(memory_space=pltpu.VMEM)
     smem = pl.BlockSpec(memory_space=pltpu.SMEM)
     return pl.pallas_call(
         functools.partial(exchange_kernel, subs, scale),
-        in_specs=[smem, smem, vmem, vmem, vmem, vmem],
+        in_specs=[smem, vmem, vmem, vmem, vmem],
         out_specs=vmem,
         out_shape=jax.ShapeDtypeStruct((children, columns), F32),
         scratch_shapes=[
             pltpu.VMEM((rows, size), F32),
             pltpu.VMEM((size, size), F32),
-            pltpu.VMEM((HALVES, zs, 2, 2) + tile, F32),
-            pltpu.VMEM((HALVES, zs, 2) + tile, F32),
-            pltpu.VMEM((HALVES, zs) + tile, F32),
-            pltpu.VMEM((max(1, zs - 1), HALVES) + tile, F32),
-            pltpu.VMEM((2, HALVES) + tile, F32),
+            pltpu.VMEM((HALVES, zs, 2, 2) + packed, F32),
+            pltpu.VMEM((HALVES, zs, 2) + packed, F32),
+            pltpu.VMEM((HALVES, zs) + packed, F32),
+            pltpu.VMEM((max(1, zs - 1), HALVES) + packed, F32),
+            pltpu.VMEM((2, HALVES) + packed, F32),
             pltpu.VMEM((HALVES,) + tile, BF16),
             pltpu.VMEM((2, HALVES, zs, 2, 2) + tile, BF16),
             pltpu.SemaphoreType.DMA((copies,)),
@@ -323,7 +363,7 @@
             collective_id=0, has_side_effects=True, vmem_limit_bytes=60 << 20
         ),
         name="exchange",
-    )(owner, row_block, grams.reshape((2, HALVES, zs, 2, 2) + tile), records, parent, eigs)
+    )(index, grams.reshape((2, HALVES, zs, 2, 2) + packed), records, parent, eigs)
 
 
 def per_device(
@@ -331,12 +371,11 @@
 ):
     subs = lax.axis_size("sub")
     parents = subs * parent_modes.shape[0]
-    records, grams = records_and_grams(
-        coupling, coupling_pairs, modes, mode_weights, parent_of, row_block, parents
-    )
+    index = jnp.concatenate([parent_of.T, row_block[None], coupling_pairs.T], axis=0)
+    records, grams = records_and_grams(index, coupling, modes, mode_weights, parents)
     scale = 1.0 / (coupling.shape[0] * modes.shape[2] * lax.axis_size("mode"))
     return strengths(
-        parent_of, row_block, grams, records, parent_modes[0], parent_eigs, subs, scale
+        index, grams, records, parent_modes[0], parent_eigs, subs, scale
     )
 
 

time: 85.1 us -> 75.8 us (0.89)
  Pallas kernels: 80.5 us -> 72.9 us
  local copies, waits for them, and re-layouts: 4.1 us -> 1.38 us
  other arithmetic: 0 us -> 1.28 us
    pallas_call x1, Pallas kernels: 68.4 us -> 62.8 us  [strengths(): pl.pallas_call(functools.partial(exchange_kernel, subs, scale), in_specs=...]
    unnamed x3 -> x1, local copies, waits for them, and re-layouts: 4.1 us -> 1.38 us
    pallas_call x1, Pallas kernels: 12.1 us -> 10.1 us  [records_and_grams(): pl.pallas_call(functools.partial(record_kernel, group, parents), grid_spe...]
    concatenate x0 -> x1, other arithmetic: none -> 1.28 us  [per_device(): jnp.concatenate([parent_of.T, row_block[None], coupling_pairs.T], axis=0)]
where the time goes in v3:
time: 75.8 us; the launch traced here: 75.6 us
  Pallas kernels  72.9 us (96%)
  local copies, waits for them, and re-layouts  1.38 us (2%)
  other arithmetic  1.28 us (2%)
    pallas_call x1, Pallas kernels, strengths(): pl.pallas_call(functools.partial(exchange_kernel, subs, scale), in_specs=...  62.8 us
    pallas_call x1, Pallas kernels, records_and_grams(): pl.pallas_call(functools.partial(record_kernel, group, parents), grid_spe...  10.1 us

profile of v3, /device:TPU:0, one launch (start us, length us, event | category | flops | bytes accessed | tf_op | source)
XLA Modules:
  0.0 75.6 jit_solution(17759211543648380578)
XLA Ops:
  0.0 1.3 %pad_add_fusion.index_ref = s32[4,64]{1,0:T(4,128)} fusion(s32[2,64]{1,0:T(2,128)} %bitcast.9, s32[1,64]{1,0:T(1,128)} %bitcast.10, s32[1,64]{1,0:T(1,128)} %bitcast.11), kind=kLoop, calls=%fused_computation | loop fusion | flops 512 | bytes 2048 | tf_op jit(solution)/shard_map/concatenate | solution.py:374
  1.3 10.1 %records.1 = (bf16[64,64,128]{2,1,0:T(8,128)(2,1)}, f32[64,40,128]{2,1,0:T(8,128)}) custom-call(s32[4,64]{1,0:T(4,128)} %pad_add_fusion.index_ref, bf16[64,64,128]{2,1,0:T(8,128)(2,1)} %coupling_ref.1, bf16[64,4,64,128]{3,2,1,0:T(8,128)(2,1)} %bitcast.6, bf16[64,128]{1,0:T(8,128)(2,1)} %weight_ref.1), custom_call_target="tpu_custom_call" | custom-call | tf_op jit(solution)/shard_map/records/pallas_call | solution.py:99
  11.4 62.8 %exchange.1 = f32[64,128]{1,0:T(8,128)} custom-call(s32[4,64]{1,0:T(4,128)} %pad_add_fusion.index_ref, f32[2,2,4,2,2,40,128]{6,5,4,3,2,1,0:T(8,128)} %bitcast.7, bf16[64,64,128]{2,1,0:T(8,128)(2,1)} %get-tuple-element.8.record_ref, bf16[512,256]{1,0:T(8,128)(2,1)} %bitcast.8, f32[1,256]{1,0:T(1,128)} %eig_ref.1), custom_call_target="tpu_custom_call" | custom-call | tf_op jit(solution)/shard_map/exchange/pallas_call | solution.py:344
  74.2 1.4 %copy.10 = f32[64,128]{1,0:T(8,128)} copy(f32[64,128]{1,0:T(8,128)} %exchange.1) | data formatting | bytes 65536

commit v4 on v3

--- a/solution.py
+++ b/solution.py
@@ -299,19 +299,23 @@
     a = spread.at[core, 0, :, y, x]
     b = spread.at[core, 1, :, y, x]
     up = [send(a, a, near_y), send(b, b, near_x)]
-    for copy in up:
-        copy.wait()
+    across = [send(a, a, sibling), send(b, b, sibling)]
     a = spread.at[core, 0, :, :, x]
     b = spread.at[core, 1, :, y]
-    last = [send(a, a, near_x), send(b, b, near_y)]
-    across = [
-        send(spread.at[core, 0, :, :, x], spread.at[core, 0, :, :, x], sibling),
-        send(spread.at[core, 1, :, y], spread.at[core, 1, :, y], sibling),
-    ]
-    for copy in last:
-        copy.wait()
-    across.append(send(spread.at[core, 0, :, :, 1 - x], spread.at[core, 0, :, :, 1 - x], sibling))
-    across.append(send(spread.at[core, 1, :, 1 - y], spread.at[core, 1, :, 1 - y], sibling))
+    last = []
+    up[0].wait()
+    last.append(send(a, a, near_x))
+    up[1].wait()
+    last.append(send(b, b, near_y))
+    a = spread.at[core, 0, :, 1 - y, x]
+    b = spread.at[core, 1, :, y, 1 - x]
+    across += [send(a, a, sibling), send(b, b, sibling)]
+    a = spread.at[core, 0, :, :, 1 - x]
+    b = spread.at[core, 1, :, 1 - y]
+    last[0].wait()
+    across.append(send(a, a, sibling))
+    last[1].wait()
+    across.append(send(b, b, sibling))
     for copy in across:
         copy.wait()
 
@@ -338,7 +342,7 @@
     zs = subs // 4
     tile = (block, 2 * block)
     packed = grams.shape[1:]
-    copies = 16 + 2 * (zs - 1)
+    copies = 20 + 2 * (zs - 1)
     vmem = pl.BlockSpec(memory_space=pltpu.VMEM)
     smem = pl.BlockSpec(memory_space=pltpu.SMEM)
     return pl.pallas_call(

time: 75.8 us -> 75.7 us (level)
  no operation moved by 1% of the time
where the time goes in v4:
time: 75.7 us; the launch traced here: 75.5 us
  Pallas kernels  72.8 us (96%)
  local copies, waits for them, and re-layouts  1.38 us (2%)
  other arithmetic  1.28 us (2%)
    pallas_call x1, Pallas kernels, strengths(): pl.pallas_call(functools.partial(exchange_kernel, subs, scale), in_specs=...  62.7 us
    pallas_call x1, Pallas kernels, records_and_grams(): pl.pallas_call(functools.partial(record_kernel, group, parents), grid_spe...  10.1 us

profile of v4, /device:TPU:0, one launch (start us, length us, event | category | flops | bytes accessed | tf_op | source)
XLA Modules:
  0.0 75.5 jit_solution(6570240332738079931)
XLA Ops:
  0.0 1.3 %pad_add_fusion.index_ref = s32[4,64]{1,0:T(4,128)} fusion(s32[2,64]{1,0:T(2,128)} %bitcast.9, s32[1,64]{1,0:T(1,128)} %bitcast.10, s32[1,64]{1,0:T(1,128)} %bitcast.11), kind=kLoop, calls=%fused_computation | loop fusion | flops 512 | bytes 2048 | tf_op jit(solution)/shard_map/concatenate | solution.py:378
  1.3 10.1 %records.1 = (bf16[64,64,128]{2,1,0:T(8,128)(2,1)}, f32[64,40,128]{2,1,0:T(8,128)}) custom-call(s32[4,64]{1,0:T(4,128)} %pad_add_fusion.index_ref, bf16[64,64,128]{2,1,0:T(8,128)(2,1)} %coupling_ref.1, bf16[64,4,64,128]{3,2,1,0:T(8,128)(2,1)} %bitcast.6, bf16[64,128]{1,0:T(8,128)(2,1)} %weight_ref.1), custom_call_target="tpu_custom_call" | custom-call | tf_op jit(solution)/shard_map/records/pallas_call | solution.py:99
  11.4 62.7 %exchange.1 = f32[64,128]{1,0:T(8,128)} custom-call(s32[4,64]{1,0:T(4,128)} %pad_add_fusion.index_ref, f32[2,2,4,2,2,40,128]{6,5,4,3,2,1,0:T(8,128)} %bitcast.7, bf16[64,64,128]{2,1,0:T(8,128)(2,1)} %get-tuple-element.8.record_ref, bf16[512,256]{1,0:T(8,128)(2,1)} %bitcast.8, f32[1,256]{1,0:T(1,128)} %eig_ref.1), custom_call_target="tpu_custom_call" | custom-call | tf_op jit(solution)/shard_map/exchange/pallas_call | solution.py:348
  74.1 1.4 %copy.10 = f32[64,128]{1,0:T(8,128)} copy(f32[64,128]{1,0:T(8,128)} %exchange.1) | data formatting | bytes 65536
